TPU v7x, 32 devices: a whole 2x2x4 slice. The times are simulated.
32 devices in a mesh: dom: 32 (over z, y, x, core).
Axes of the slice: x: 2, y: 2, z: 4, core: 2. Of those that a mesh axis runs over, the one named last changes fastest.
Arguments:
- z_state: bfloat16 [96, 262144], P(None, 'dom'), may hold values from 0 to 20, as said below
- inputs: bfloat16 [128, 262144], P(None, 'dom'), may hold values from -6 to 6
- adjoint: bfloat16 [96, 262144], P(None, 'dom'), may hold values from -6 to 6
- cotangent: bfloat16 [96, 262144], P(None, 'dom'), may hold values from -0.59765625 to 0.59765625
- mix_weight: bfloat16 [96, 96], replicated, may hold values from -0.625 to 0.625
- input_weight: bfloat16 [96, 128], replicated, may hold values from -0.5 to 0.5
- tile_values: bfloat16 [8192, 128, 128], P('dom'), may hold values from 0 to 0.019897461
- tile_src: int32 [32, 256], P('dom'), may hold values from 0 to 191, as said below
- tile_dst: int32 [32, 256], P('dom'), may hold values from 0 to 63
- send_list: int32 [32, 8, 16], P('dom'), may hold values from 0 to 63
Outputs:
- fixed_next: bfloat16 [96, 262144], P(None, 'dom')
- adjoint_next: bfloat16 [96, 262144], P(None, 'dom')
- weight_grad: float32 [96, 96], replicated
- input_grad: float32 [96, 128], replicated
Inputs may be any that keep to these rules, and one draw needn't show every extreme that they name: `tile_src`: codes below 64 name a local tile; code 64 + o * 16 + c names slot c of neighbour o's list for this partition. Every code from 64 upward appears on every partition. `z_state`: zero or positive; a state after a rectifier.
All inputs are finite; a program needn't handle non-finite values.
Results may differ from a plain program's by a relative error of at most 0.0058.
Values may be sent and summed in bfloat16 or wider, within the bound.
A program may use at most 128 MiB of HBM per device.

v0:
```python
import math

import jax
import jax.numpy as jnp
from jax import lax
from jax.sharding import PartitionSpec as P


def shifted(array, axis, by):
    devices = lax.axis_size(axis)
    return lax.ppermute(array, axis, [(i, (i + by) % devices) for i in range(devices)])


def offset_list(reach_count):
    return [reach_step + 1 for reach_step in range(reach_count)] + [
        -(reach_step + 1) for reach_step in range(reach_count)
    ]


def group_rows(values, member_ids, group_count):
    onehot = (member_ids[None, :] == jnp.arange(group_count, dtype=jnp.int32)[:, None]).astype(
        jnp.float32
    )
    flat = values.reshape(values.shape[0], -1)
    grouped = jnp.dot(
        onehot, flat, precision=lax.Precision.HIGHEST, preferred_element_type=jnp.float32
    )
    return grouped.reshape((group_count,) + values.shape[1:])


def per_device(
    z_state,
    inputs,
    adjoint,
    cotangent,
    mix_weight,
    input_weight,
    tile_values,
    tile_src,
    tile_dst,
    send_list,
):
    channels, node_rows = z_state.shape
    tile_size = tile_values.shape[1]
    local_tiles = node_rows // tile_size
    axis_size = lax.axis_size("dom")
    send_ids = send_list[0]
    peer_slots, capacity = send_ids.shape
    reach_count = peer_slots // 2
    offsets = offset_list(reach_count)
    sources = tile_src[0]
    targets = tile_dst[0]
    state_tiles = z_state.reshape(channels, local_tiles, tile_size)
    outgoing = state_tiles[:, send_ids.reshape(-1)].reshape(
        channels, peer_slots, capacity, tile_size
    )
    arrivals = []
    for offset_index, shift_by in enumerate(offsets):
        arrivals.append(shifted(outgoing[:, offset_index], "dom", shift_by))
    arrived = jnp.stack(arrivals, axis=1)
    lookup_table = jnp.concatenate(
        [state_tiles, arrived.reshape(channels, peer_slots * capacity, tile_size)], axis=1
    )
    pieces = lookup_table[:, sources]
    contributions = jnp.einsum(
        "hks,ksd->khd", pieces, tile_values, preferred_element_type=jnp.float32
    )
    summed_rows = group_rows(contributions, targets, local_tiles)
    aggregated = jnp.moveaxis(summed_rows, 1, 0).reshape(channels, node_rows).astype(jnp.bfloat16)
    preactivation = jnp.dot(mix_weight, aggregated, preferred_element_type=jnp.float32) + jnp.dot(
        input_weight, inputs, preferred_element_type=jnp.float32
    )
    fixed_next = jnp.maximum(preactivation, 0.0).astype(jnp.bfloat16)
    masked = jnp.where(z_state > 0, adjoint, jnp.zeros_like(adjoint))
    backward = lax.dot_general(
        mix_weight, masked, (((0,), (0,)), ((), ())), preferred_element_type=jnp.float32
    ).astype(jnp.bfloat16)
    back_pieces = backward.reshape(channels, local_tiles, tile_size)[:, targets]
    partials = jnp.einsum(
        "hkd,ksd->khs", back_pieces, tile_values, preferred_element_type=jnp.float32
    )
    code_count = local_tiles + peer_slots * capacity
    by_code = jnp.moveaxis(group_rows(partials, sources, code_count), 1, 0)
    local_sum = by_code[:, :local_tiles]
    leaving = by_code[:, local_tiles:].reshape(channels, peer_slots, capacity, tile_size)
    returns = []
    for offset_index, shift_by in enumerate(offsets):
        returns.append(shifted(leaving[:, offset_index], "dom", -shift_by))
    returned = jnp.stack(returns, axis=1)
    returned_rows = jnp.moveaxis(returned.reshape(channels, peer_slots * capacity, tile_size), 1, 0)
    owner_sum = jnp.moveaxis(group_rows(returned_rows, send_ids.reshape(-1), local_tiles), 1, 0)
    adjoint_sum = (local_sum + owner_sum).reshape(channels, node_rows)
    adjoint_next = (cotangent.astype(jnp.float32) + adjoint_sum).astype(jnp.bfloat16)
    local_weight = lax.dot_general(
        masked, aggregated, (((1,), (1,)), ((), ())), preferred_element_type=jnp.float32
    )
    local_input = lax.dot_general(
        masked, inputs, (((1,), (1,)), ((), ())), preferred_element_type=jnp.float32
    )
    weight_total, input_total = lax.psum((local_weight, local_input), "dom")
    normalizer = 1.0 / math.sqrt(node_rows * axis_size)
    return (fixed_next, adjoint_next, weight_total * normalizer, input_total * normalizer)


def solution(mesh):
    return jax.shard_map(
        per_device,
        mesh=mesh,
        in_specs=(
            P(None, "dom"),
            P(None, "dom"),
            P(None, "dom"),
            P(None, "dom"),
            P(),
            P(),
            P("dom", None, None),
            P("dom", None),
            P("dom", None),
            P("dom", None, None),
        ),
        out_specs=(P(None, "dom"), P(None, "dom"), P(), P()),
        check_vma=False,
    )
```

profile of v0, /device:TPU:2, one launch (start us, length us, event | category | flops | bytes accessed | tf_op | source)
XLA Modules:
  0.0 479.5 jit_solution(5482104733957202202)
XLA Ops:
  8.7 2.5 fusion.14
  12.7 5.4 %gather_fusion.2 = bf16[256,96,128]{2,1,0:T(8,128)(2,1)} fusion(bf16[96,64,128]{2,0,1:T(8,128)(2,1)} %bitcast.190, s32[1024]{0:T(1024)S(1)} %get-tuple-element.22), kind=kCustom, calls=%fused_computation.2 | custom fusion | bytes 12583936 | tf_op jit(solution)/shard_map/gather | solution.py:78
  18.0 15.6 %fusion.4 = f32[256,96,128]{2,1,0:T(8,128)} fusion(bf16[256,128,128]{2,1,0:T(8,128)(2,1)} %param.16, bf16[256,96,128]{2,1,0:T(8,128)(2,1)} %gather_fusion.2), kind=kOutput, calls=%fused_computation.12 | convolution fusion | flops 805306368 | bytes 27262976 | tf_op jit(solution)/shard_map/hkd,ksd->khs/dot_general | solution.py:79
  33.7 20.8 %copy.116 = f32[32,8,96,128]{3,1,2,0:T(8,128)} copy(f32[32,8,96,128]{3,2,1,0:T(8,128)} %bitcast.188) | data formatting | bytes 25165824
  54.5 12.6 %copy.63 = f32[12288,256]{1,0:T(8,128)} copy(f32[12288,256]{0,1:T(8,128)} %bitcast.185) | data formatting | bytes 25165824 | tf_op jit(solution)/shard_map/dot_general | solution.py:25
  67.1 9.9 %convolution_bitcast_fusion.1 = f32[96,192,128]{2,1,0:T(8,128)S(1)} fusion(f32[96,128,256]{2,1,0:T(8,128)} %bitcast.189, s32[256]{0:T(256)S(1)} %bitcast.203), kind=kOutput, calls=%fused_computation.17 | convolution fusion | flops 7247806464 | bytes 22021120 | tf_op jit(solution)/shard_map/dot_general | solution.py:25
  77.8 2.8 copy-done.1
  80.6 2.7 slice_bitcast_fusion
  83.2 5.5 %collective-permute-start.9 = (f32[96,16,128]{2,1,0:T(8,128)}, f32[96,16,128]{2,1,0:T(8,128)}, u32[]{:S(2)}, u32[]{:S(2)}) collective-permute-start(f32[96,16,128]{2,1,0:T(8,128)} %get-tuple-element.12), channel_id=1, source_target_pairs={{0,30},{1,31},{2,0},{3,1},{4,2},{5,3},{6,4},{7,5},{8,6},{9,7},{10,... | collective-permute-start | bytes 2359304 | tf_op jit(solution)/shard_map/ppermute | solution.py:11
  90.2 4.0 gather_fusion
  94.2 3.1 fusion.28
  99.8 2.4 collective-permute-start.1
  102.2 1.6 fusion.27
  107.8 27.0 %collective-permute-done = bf16[96,16,128]{2,1,0:T(8,128)(2,1)} collective-permute-done((bf16[96,16,128]{2,1,0:T(8,128)(2,1)}, bf16[96,16,128]{2,1,0:T(8,128)(2,1)}, u32[]{:S(2)}, u32[]{:S(2)}) %collective-permute-start) | collective-permute-done | bytes 393248 | tf_op jit(solution)/shard_map/ppermute | solution.py:11
  137.8 11.1 %collective-permute-done.2 = bf16[96,16,128]{2,1,0:T(8,128)(2,1)S(1)} collective-permute-done((bf16[96,16,128]{2,1,0:T(8,128)(2,1)S(1)}, bf16[96,16,128]{2,1,0:T(8,128)(2,1)S(1)}, u32[]{:S(2)}, u32[]{:S(2)}) %collective-permute-start.2) | collective-permute-done | bytes 393248 | tf_op jit(solution)/shard_map/ppermute | solution.py:11
  148.9 3.9 collective-permute-start.4
  152.9 3.0 collective-permute-done.3
  156.0 2.6 collective-permute-done.4
  158.6 4.1 collective-permute-start.6
  162.8 7.0 %collective-permute-done.5 = bf16[96,16,128]{2,1,0:T(8,128)(2,1)S(1)} collective-permute-done((bf16[96,16,128]{2,1,0:T(8,128)(2,1)S(1)}, bf16[96,16,128]{2,1,0:T(8,128)(2,1)S(1)}, u32[]{:S(2)}, u32[]{:S(2)}) %collective-permute-start.5) | collective-permute-done | bytes 393248 | tf_op jit(solution)/shard_map/ppermute | solution.py:11
  169.8 3.2 collective-permute-start.7
  173.6 11.0 %collective-permute-start.11 = (f32[96,16,128]{2,1,0:T(8,128)}, f32[96,16,128]{2,1,0:T(8,128)}, u32[]{:S(2)}, u32[]{:S(2)}) collective-permute-start(f32[96,16,128]{2,1,0:T(8,128)} %get-tuple-element.10), channel_id=1, source_target_pairs={{0,28},{1,29},{2,30},{3,31},{4,0},{5,1},{6,2},{7,3},{8,4},{9,5},{1... | collective-permute-start | bytes 2359304 | tf_op jit(solution)/shard_map/ppermute | solution.py:11
  184.6 3.2 collective-permute-done.7
  188.0 2.0 copy.60
  190.1 2.6 pad_maximum_fusion
  192.7 6.3 %gather_fusion.1 = bf16[256,96,128]{2,1,0:T(8,128)(2,1)} fusion(bf16[96,192,128]{2,0,1:T(8,128)(2,1)} %pad_maximum_fusion, s32[1024]{0:T(1024)S(1)} %get-tuple-element.23), kind=kCustom, calls=%fused_computation.1 | custom fusion | bytes 12583936 | tf_op jit(solution)/shard_map/gather | solution.py:64
  199.0 12.0 %fusion.6 = f32[256,96,128]{2,1,0:T(8,128)} fusion(bf16[256,128,128]{2,1,0:T(8,128)(2,1)} %param.16, bf16[256,96,128]{2,1,0:T(8,128)(2,1)} %gather_fusion.1), kind=kOutput, calls=%fused_computation.14 | convolution fusion | flops 805306368 | bytes 27262976 | tf_op jit(solution)/shard_map/hks,ksd->khd/dot_general | solution.py:65
  211.0 20.6 %copy.117 = f32[32,8,96,128]{3,1,2,0:T(8,128)} copy(f32[32,8,96,128]{3,2,1,0:T(8,128)} %bitcast.184) | data formatting | bytes 25165824
  231.6 12.6 %copy.61 = f32[12288,256]{1,0:T(8,128)} copy(f32[12288,256]{0,1:T(8,128)} %bitcast.186) | data formatting | bytes 25165824 | tf_op jit(solution)/shard_map/dot_general | solution.py:25
  244.3 10.6 %convolution_convert_fusion.1 = bf16[64,96,128]{2,0,1:T(8,128)(2,1)S(1)} fusion(f32[96,128,256]{2,1,0:T(8,128)} %bitcast.187, s32[256]{0:T(256)S(1)} %bitcast.204), kind=kOutput, calls=%fused_computation.22 | convolution fusion | flops 2416721920 | bytes 14156800 | tf_op jit(solution)/shard_map/dot_general | solution.py:25
  256.1 1.8 fusion.11
  257.9 4.3 convolution_bitcast_fusion
  262.3 3.6 fusion.1
  265.9 120.4 %all-reduce.3.cloned.1.call-done = (f32[96,96]{1,0:T(8,128)}, f32[96,128]{1,0:T(8,128)}) async-done(((f32[96,96]{1,0:T(8,128)}, f32[96,128]{1,0:T(8,128)}), (f32[96,96]{1,0:T(8,128)}, f32[96,128]{1,0:T(8,128)})) %all-reduce.3.cloned.1.call-update) | async-done | bytes 86032 | tf_op jit(solution)/shard_map/psum | solution.py:100
  386.3 1.4 broadcast_multiply_fusion
  389.1 1.4 collective-permute-start.13
  390.6 2.1 bitcast_dynamic-update-slice_fusion.7
  392.7 2.1 bitcast_dynamic-update-slice_fusion.6
  394.8 3.4 collective-permute-start.15
  398.2 2.2 bitcast_dynamic-update-slice_fusion.5
  400.4 2.1 bitcast_dynamic-update-slice_fusion.4
  402.5 2.1 bitcast_dynamic-update-slice_fusion.3
  404.6 3.4 collective-permute-done.13
  409.0 25.8 %collective-permute-done.14 = f32[96,16,128]{2,1,0:T(8,128)S(1)} collective-permute-done((f32[96,16,128]{2,1,0:T(8,128)}, f32[96,16,128]{2,1,0:T(8,128)S(1)}, u32[]{:S(2)}, u32[]{:S(2)}) %collective-permute-start.14) | collective-permute-done | bytes 786464 | tf_op jit(solution)/shard_map/ppermute | solution.py:11
  435.9 17.8 %collective-permute-done.15 = f32[96,16,128]{2,1,0:T(8,128)S(1)} collective-permute-done((f32[96,16,128]{2,1,0:T(8,128)S(1)}, f32[96,16,128]{2,1,0:T(8,128)S(1)}, u32[]{:S(2)}, u32[]{:S(2)}) %collective-permute-start.15) | collective-permute-done | bytes 786464 | tf_op jit(solution)/shard_map/ppermute | solution.py:11
  454.8 6.8 %copy.72 = f32[128,96,128]{0,2,1:T(8,128)} copy(f32[128,96,128]{2,0,1:T(8,128)} %bitcast.58) | data formatting | bytes 12582912 | tf_op jit(solution)/shard_map/transpose | solution.py:90
  461.6 7.6 %slice_add_fusion = f32[96,64,128]{2,1,0:T(8,128)S(1)} fusion(f32[96,192,128]{2,1,0:T(8,128)} %copy-done.1, f32[128,96,128]{0,2,1:T(8,128)} %copy.72, s32[128]{0:T(128)S(1)} %eq.53), kind=kOutput, calls=%fused_computation.20 | convolution fusion | flops 1208754176 | bytes 12583424 | tf_op jit(solution)/shard_map/dot_general | solution.py:25
  469.2 2.9 fusion.8
  (78 shorter events, 21.6 us)
Async XLA Ops:
  7.2 95.0 %copy-start = (bf16[128,8192]{1,0:T(8,128)(2,1)S(1)}, bf16[128,8192]{1,0:T(8,128)(2,1)}, u32[]{:S(2)}) copy-start(bf16[128,8192]{1,0:T(8,128)(2,1)} %param.11) | copy-start | bytes 6291460
  7.2 379.1 %all-reduce.3.cloned.1.call-start = ((), (), s32[]{:S(2)}) async-start(), calls=%async_computation | async-start | bytes 196608 | tf_op jit(solution)/shard_map/psum | solution.py:100
  54.4 12.6 %copy-start.14 = (s32[1,256]{1,0:T(1,128)S(1)}, s32[1,256]{1,0:T(1,128)}, u32[]{:S(2)}) copy-start(s32[1,256]{1,0:T(1,128)} %param.17) | copy-start | bytes 3076
  77.0 3.6 copy-start.1
  80.6 8.1 %copy-start.4 = (bf16[96,8192]{1,0:T(8,128)(2,1)S(1)}, bf16[96,8192]{1,0:T(8,128)(2,1)}, u32[]{:S(2)}) copy-start(bf16[96,8192]{1,0:T(8,128)(2,1)} %param.10) | copy-start | bytes 4718596
  83.2 6.9 %copy-start.13 = (s32[1,8,16]{2,1,0:T(8,128)S(1)}, s32[1,8,16]{2,1,0:T(8,128)}, u32[]{:S(2)}) copy-start(s32[1,8,16]{2,1,0:T(8,128)} %param.19) | copy-start | bytes 1540
  83.2 305.9 %collective-permute-start.8 = (f32[96,16,128]{2,1,0:T(8,128)}, f32[96,16,128]{2,1,0:T(8,128)}, u32[]{:S(2)}, u32[]{:S(2)}) collective-permute-start(f32[96,16,128]{2,1,0:T(8,128)} %get-tuple-element.13), channel_id=1, source_target_pairs={{0,31},{1,0},{2,1},{3,2},{4,3},{5,4},{6,5},{7,6},{8,7},{9,8},{10,9... | collective-permute-start | bytes 2359304 | tf_op jit(solution)/shard_map/ppermute | solution.py:11
  83.2 309.4 %collective-permute-start.9 = (f32[96,16,128]{2,1,0:T(8,128)}, f32[96,16,128]{2,1,0:T(8,128)}, u32[]{:S(2)}, u32[]{:S(2)}) collective-permute-start(f32[96,16,128]{2,1,0:T(8,128)} %get-tuple-element.12), channel_id=1, source_target_pairs={{0,30},{1,31},{2,0},{3,1},{4,2},{5,3},{6,4},{7,5},{8,6},{9,7},{10,... | collective-permute-start | bytes 2359304 | tf_op jit(solution)/shard_map/ppermute | solution.py:11
  88.7 306.1 %collective-permute-start.10 = (f32[96,16,128]{2,1,0:T(8,128)}, f32[96,16,128]{2,1,0:T(8,128)}, u32[]{:S(2)}, u32[]{:S(2)}) collective-permute-start(f32[96,16,128]{2,1,0:T(8,128)} %get-tuple-element.11), channel_id=1, source_target_pairs={{0,29},{1,30},{2,31},{3,0},{4,1},{5,2},{6,3},{7,4},{8,5},{9,6},{10... | collective-permute-start | bytes 2359304 | tf_op jit(solution)/shard_map/ppermute | solution.py:11
  94.2 8.0 %copy-start.5 = (bf16[96,8192]{1,0:T(8,128)(2,1)S(1)}, bf16[96,8192]{1,0:T(8,128)(2,1)}, u32[]{:S(2)}) copy-start(bf16[96,8192]{1,0:T(8,128)(2,1)} %param.10) | copy-start | bytes 4718596
  94.2 8.0 %copy-start.7 = (bf16[96,8192]{1,0:T(8,128)(2,1)S(1)}, bf16[96,8192]{1,0:T(8,128)(2,1)}, u32[]{:S(2)}) copy-start(bf16[96,8192]{1,0:T(8,128)(2,1)} %param.12) | copy-start | bytes 4718596
  98.2 36.6 %collective-permute-start = (bf16[96,16,128]{2,1,0:T(8,128)(2,1)}, bf16[96,16,128]{2,1,0:T(8,128)(2,1)}, u32[]{:S(2)}, u32[]{:S(2)}) collective-permute-start(bf16[96,16,128]{2,1,0:T(8,128)(2,1)} %bitcast.183), channel_id=1, source_target_pairs={{0,1},{1,2},{2,3},{3,4},{4,5},{5,6},{6,7},{7,8},{8,9},{9,10},{10,1... | collective-permute-start | bytes 1179656 | tf_op jit(solution)/shard_map/ppermute | solution.py:11
  99.8 36.9 %collective-permute-start.1 = (bf16[96,16,128]{2,1,0:T(8,128)(2,1)}, bf16[96,16,128]{2,1,0:T(8,128)(2,1)}, u32[]{:S(2)}, u32[]{:S(2)}) collective-permute-start(bf16[96,16,128]{2,1,0:T(8,128)(2,1)} %bitcast.182), channel_id=1, source_target_pairs={{0,2},{1,3},{2,4},{3,5},{4,6},{5,7},{6,8},{7,9},{8,10},{9,11},{10,... | collective-permute-start | bytes 1179656 | tf_op jit(solution)/shard_map/ppermute | solution.py:11
  134.8 14.1 %collective-permute-start.2 = (bf16[96,16,128]{2,1,0:T(8,128)(2,1)S(1)}, bf16[96,16,128]{2,1,0:T(8,128)(2,1)S(1)}, u32[]{:S(2)}, u32[]{:S(2)}) collective-permute-start(bf16[96,16,128]{2,1,0:T(8,128)(2,1)S(1)} %bitcast.202), channel_id=1, source_target_pairs={{0,3},{1,4},{2,5},{3,6},{4,7},{5,8},{6,9},{7,10},{8,11},{9,12},{10... | collective-permute-start | bytes 1179656 | tf_op jit(solution)/shard_map/ppermute | solution.py:11
  136.7 19.2 %collective-permute-start.3 = (bf16[96,16,128]{2,1,0:T(8,128)(2,1)S(1)}, bf16[96,16,128]{2,1,0:T(8,128)(2,1)S(1)}, u32[]{:S(2)}, u32[]{:S(2)}) collective-permute-start(bf16[96,16,128]{2,1,0:T(8,128)(2,1)S(1)} %bitcast.201), channel_id=1, source_target_pairs={{0,4},{1,5},{2,6},{3,7},{4,8},{5,9},{6,10},{7,11},{8,12},{9,13},{1... | collective-permute-start | bytes 1179656 | tf_op jit(solution)/shard_map/ppermute | solution.py:11
  148.9 9.7 %collective-permute-start.4 = (bf16[96,16,128]{2,1,0:T(8,128)(2,1)S(1)}, bf16[96,16,128]{2,1,0:T(8,128)(2,1)S(1)}, u32[]{:S(2)}, u32[]{:S(2)}) collective-permute-start(bf16[96,16,128]{2,1,0:T(8,128)(2,1)S(1)} %bitcast.200), channel_id=1, source_target_pairs={{0,31},{1,0},{2,1},{3,2},{4,3},{5,4},{6,5},{7,6},{8,7},{9,8},{10,9... | collective-permute-start | bytes 1179656 | tf_op jit(solution)/shard_map/ppermute | solution.py:11
  155.9 13.9 %collective-permute-start.5 = (bf16[96,16,128]{2,1,0:T(8,128)(2,1)S(1)}, bf16[96,16,128]{2,1,0:T(8,128)(2,1)S(1)}, u32[]{:S(2)}, u32[]{:S(2)}) collective-permute-start(bf16[96,16,128]{2,1,0:T(8,128)(2,1)S(1)} %bitcast.199), channel_id=1, source_target_pairs={{0,30},{1,31},{2,0},{3,1},{4,2},{5,3},{6,4},{7,5},{8,6},{9,7},{10,... | collective-permute-start | bytes 1179656 | tf_op jit(solution)/shard_map/ppermute | solution.py:11
  158.6 14.9 %collective-permute-start.6 = (bf16[96,16,128]{2,1,0:T(8,128)(2,1)S(1)}, bf16[96,16,128]{2,1,0:T(8,128)(2,1)S(1)}, u32[]{:S(2)}, u32[]{:S(2)}) collective-permute-start(bf16[96,16,128]{2,1,0:T(8,128)(2,1)S(1)} %bitcast.198), channel_id=1, source_target_pairs={{0,29},{1,30},{2,31},{3,0},{4,1},{5,2},{6,3},{7,4},{8,5},{9,6},{10... | collective-permute-start | bytes 1179656 | tf_op jit(solution)/shard_map/ppermute | solution.py:11
  169.8 18.0 %collective-permute-start.7 = (bf16[96,16,128]{2,1,0:T(8,128)(2,1)S(1)}, bf16[96,16,128]{2,1,0:T(8,128)(2,1)S(1)}, u32[]{:S(2)}, u32[]{:S(2)}) collective-permute-start(bf16[96,16,128]{2,1,0:T(8,128)(2,1)S(1)} %bitcast.197), channel_id=1, source_target_pairs={{0,28},{1,29},{2,30},{3,31},{4,0},{5,1},{6,2},{7,3},{8,4},{9,5},{1... | collective-permute-start | bytes 1179656 | tf_op jit(solution)/shard_map/ppermute | solution.py:11
  173.6 226.8 %collective-permute-start.11 = (f32[96,16,128]{2,1,0:T(8,128)}, f32[96,16,128]{2,1,0:T(8,128)}, u32[]{:S(2)}, u32[]{:S(2)}) collective-permute-start(f32[96,16,128]{2,1,0:T(8,128)} %get-tuple-element.10), channel_id=1, source_target_pairs={{0,28},{1,29},{2,30},{3,31},{4,0},{5,1},{6,2},{7,3},{8,4},{9,5},{1... | collective-permute-start | bytes 2359304 | tf_op jit(solution)/shard_map/ppermute | solution.py:11
  187.8 214.7 %collective-permute-start.12 = (f32[96,16,128]{2,1,0:T(8,128)}, f32[96,16,128]{2,1,0:T(8,128)}, u32[]{:S(2)}, u32[]{:S(2)}) collective-permute-start(f32[96,16,128]{2,1,0:T(8,128)} %get-tuple-element.9), channel_id=1, source_target_pairs={{0,1},{1,2},{2,3},{3,4},{4,5},{5,6},{6,7},{7,8},{8,9},{9,10},{10,1... | collective-permute-start | bytes 2359304 | tf_op jit(solution)/shard_map/ppermute | solution.py:11
  188.0 2.0 copy-start.2
  231.6 12.6 %copy-start.15 = (s32[1,256]{1,0:T(1,128)S(1)}, s32[1,256]{1,0:T(1,128)}, u32[]{:S(2)}) copy-start(s32[1,256]{1,0:T(1,128)} %param.18) | copy-start | bytes 3076
  244.3 11.8 %copy-start.6 = (bf16[96,8192]{1,0:T(8,128)(2,1)S(1)}, bf16[96,8192]{1,0:T(8,128)(2,1)}, u32[]{:S(2)}) copy-start(bf16[96,8192]{1,0:T(8,128)(2,1)} %param.10) | copy-start | bytes 4718596
  244.3 11.8 %copy-start.8 = (bf16[96,8192]{1,0:T(8,128)(2,1)S(1)}, bf16[96,8192]{1,0:T(8,128)(2,1)}, u32[]{:S(2)}) copy-start(bf16[96,8192]{1,0:T(8,128)(2,1)} %param.12) | copy-start | bytes 4718596
  254.9 1.1 copy-start.3
  256.1 1.9 copy-start.11
  257.9 4.3 copy-start.12
  265.9 128.9 %copy-start.10 = (f32[96,16,128]{2,1,0:T(8,128)S(1)}, f32[96,16,128]{2,1,0:T(8,128)}, u32[]{:S(2)}) copy-start(f32[96,16,128]{2,1,0:T(8,128)} %get-tuple-element.6) | copy-start | bytes 2359300
  389.1 18.8 %collective-permute-start.13 = (f32[96,16,128]{2,1,0:T(8,128)}, f32[96,16,128]{2,1,0:T(8,128)S(1)}, u32[]{:S(2)}, u32[]{:S(2)}) collective-permute-start(f32[96,16,128]{2,1,0:T(8,128)} %get-tuple-element.8), channel_id=1, source_target_pairs={{0,2},{1,3},{2,4},{3,5},{4,6},{5,7},{6,8},{7,9},{8,10},{9,11},{10,... | collective-permute-start | bytes 2359304 | tf_op jit(solution)/shard_map/ppermute | solution.py:11
  392.7 42.2 %collective-permute-start.14 = (f32[96,16,128]{2,1,0:T(8,128)}, f32[96,16,128]{2,1,0:T(8,128)S(1)}, u32[]{:S(2)}, u32[]{:S(2)}) collective-permute-start(f32[96,16,128]{2,1,0:T(8,128)} %get-tuple-element.7), channel_id=1, source_target_pairs={{0,3},{1,4},{2,5},{3,6},{4,7},{5,8},{6,9},{7,10},{8,11},{9,12},{10... | collective-permute-start | bytes 2359304 | tf_op jit(solution)/shard_map/ppermute | solution.py:11
  394.8 58.9 %collective-permute-start.15 = (f32[96,16,128]{2,1,0:T(8,128)S(1)}, f32[96,16,128]{2,1,0:T(8,128)S(1)}, u32[]{:S(2)}, u32[]{:S(2)}) collective-permute-start(f32[96,16,128]{2,1,0:T(8,128)S(1)} %copy-done.10), channel_id=1, source_target_pairs={{0,4},{1,5},{2,6},{3,7},{4,8},{5,9},{6,10},{7,11},{8,12},{9,13},{1... | collective-permute-start | bytes 2359304 | tf_op jit(solution)/shard_map/ppermute | solution.py:11
  461.6 7.6 %copy-start.9 = (bf16[96,8192]{1,0:T(8,128)(2,1)S(1)}, bf16[96,8192]{1,0:T(8,128)(2,1)}, u32[]{:S(2)}) copy-start(bf16[96,8192]{1,0:T(8,128)(2,1)} %param.13) | copy-start | bytes 4718596
Sparse Core Ops, SparseCore 0:
  262.4 123.8 all-reduce.2
where the time goes:
time: 489 us; the launch traced here: 479 us
  waiting for transfers between devices  223 us (46%)
  local copies, waits for them, and re-layouts  127 us (26%)
  matrix products  69.7 us (14%)
  starting transfers between devices  35.7 us (7%)
  between operations  14.7 us (3%)
  other arithmetic  9.87 us (2%)
    psum x1, waiting for transfers between devices, per_device(): weight_total, input_total = lax.psum((local_weight, local_input), 'dom')  120 us
    ppermute x16, waiting for transfers between devices, shifted(): lax.ppermute(array, axis, [(i, (i + by) % devices) for i in range(devices)])  102 us
    unnamed x56, local copies, waits for them, and re-layouts  66.3 us
    ppermute x16, starting transfers between devices, shifted(): lax.ppermute(array, axis, [(i, (i + by) % devices) for i in range(devices)])  35.7 us
    dot_general x3, matrix products, group_rows(): jnp.dot(onehot, flat, precision=lax.Precision.HIGHEST, preferred_element_...  28.2 us
    dot_general x2, local copies, waits for them, and re-layouts, group_rows(): jnp.dot(onehot, flat, precision=lax.Precision.HIGHEST, preferred_element_...  25.3 us
    dot_general x1, matrix products, per_device(): jnp.einsum('hkd,ksd->khs', back_pieces, tile_values, preferred_element_ty...  15.6 us
    dot_general x1, matrix products, per_device(): jnp.einsum('hks,ksd->khd', pieces, tile_values, preferred_element_type=jn...  12 us
  transfers between devices with their start and end apart: 17, of which 12 were waited for; matrix products, arithmetic and copies ran while one was open for 23% of the time, Pallas kernels for 0%

commit v1 on v0

v1 whole, which is shorter than its diff:
```python
import functools
import math

import jax
import jax.numpy as jnp
from jax import lax
from jax.experimental import pallas as pl
from jax.experimental.pallas import tpu as pltpu
from jax.sharding import PartitionSpec as P

MESH = pl.DeviceIdType.MESH
BLOCK = 16
LANES = 1024


def lane_slice(start, size):
    return pl.ds(pl.multiple_of(start, size), size)


def dot(a, b, contract):
    return lax.dot_general(a, b, (contract, ((), ())), preferred_element_type=jnp.float32)


def backward_kernel(
    src, dst, send, z_ref, adj_ref, x_ref, w_ref, a_ref,
    zout_ref, leave_ref, local_ref, ig_ref, back, acc,
):
    step = pl.program_id(0)
    tile = a_ref.shape[1]
    nodes = z_ref.shape[1]
    slots = zout_ref.shape[0]
    local_tiles = local_ref.shape[0]

    @pl.when(step == 0)
    def _():
        def gather(s, c):
            zout_ref[s] = z_ref[:, lane_slice(send[s] * tile, tile)]
            return c

        lax.fori_loop(0, slots, gather, 0)

        def clear(s, c):
            acc[s] = jnp.zeros(acc.shape[1:], acc.dtype)
            return c

        lax.fori_loop(0, acc.shape[0], clear, 0)
        ig_ref[...] = jnp.zeros_like(ig_ref)

        def chunk(i, c):
            at = lane_slice(i * LANES, LANES)
            adj = adj_ref[:, at]
            masked = jnp.where(z_ref[:, at] > 0, adj, jnp.zeros_like(adj))
            back[:, at] = dot(w_ref[...], masked, ((0,), (0,))).astype(back.dtype)
            ig_ref[...] += dot(masked, x_ref[:, at], ((1,), (1,)))
            return c

        lax.fori_loop(0, nodes // LANES, chunk, 0)

    for j in range(a_ref.shape[0]):
        k = step * a_ref.shape[0] + j
        piece = back[:, lane_slice(dst[k] * tile, tile)]
        acc[src[k]] += dot(piece, a_ref[j], ((1,), (1,)))

    @pl.when(step == pl.num_programs(0) - 1)
    def _():
        def keep(t, c):
            local_ref[t] = acc[t]
            return c

        lax.fori_loop(0, local_tiles, keep, 0)

        def leave(s, c):
            leave_ref[s] = acc[local_tiles + s].astype(leave_ref.dtype)
            return c

        lax.fori_loop(0, slots, leave, 0)


def exchange_kernel(n, offsets, zout, leave, zin, ret, send_sem, recv_sem):
    me = lax.axis_index("dom")
    barrier = pltpu.get_barrier_semaphore()
    for off in offsets:
        pl.semaphore_signal(
            barrier, inc=1, device_id=(lax.rem(me + off + n, n),), device_id_type=MESH
        )
    pl.semaphore_wait(barrier, len(offsets))
    cap = zout.shape[0] // len(offsets)
    copies = []
    for kind, (src, dst, sign) in enumerate(((zout, zin, 1), (leave, ret, -1))):
        for o, off in enumerate(offsets):
            at = pl.ds(o * cap, cap)
            copies.append(
                pltpu.make_async_remote_copy(
                    src_ref=src.at[at],
                    dst_ref=dst.at[at],
                    send_sem=send_sem.at[kind, o],
                    recv_sem=recv_sem.at[kind, o],
                    device_id=(lax.rem(me + sign * off + n, n),),
                    device_id_type=MESH,
                )
            )
    for copy in copies:
        copy.start()
    for copy in copies:
        copy.wait()


def forward_kernel(
    src, dst, send, z_ref, adj_ref, cot_ref, x_ref, w_ref, b_ref, zin_ref, ret_ref, local_ref,
    a_ref, fixed_ref, next_ref, wg_ref, table, acc, own,
):
    step = pl.program_id(0)
    tile = a_ref.shape[1]
    nodes = z_ref.shape[1]
    slots = zin_ref.shape[0]
    local_tiles = acc.shape[0]

    @pl.when(step == 0)
    def _():
        def fill(t, c):
            at = lane_slice(t * tile, tile)
            table[t] = z_ref[:, at]
            acc[t] = jnp.zeros(acc.shape[1:], acc.dtype)
            own[t] = local_ref[t] + cot_ref[:, at].astype(jnp.float32)
            return c

        lax.fori_loop(0, local_tiles, fill, 0)

        def fill_in(s, c):
            table[local_tiles + s] = zin_ref[s]
            own[send[s]] += ret_ref[s].astype(jnp.float32)
            return c

        lax.fori_loop(0, slots, fill_in, 0)

    for j in range(a_ref.shape[0]):
        k = step * a_ref.shape[0] + j
        acc[dst[k]] += dot(table[src[k]], a_ref[j], ((1,), (0,)))

    @pl.when(step == pl.num_programs(0) - 1)
    def _():
        per = LANES // tile
        wg_ref[...] = jnp.zeros_like(wg_ref)

        def chunk(i, c):
            at = lane_slice(i * LANES, LANES)
            agg = jnp.concatenate(
                [acc[i * per + p].astype(jnp.bfloat16) for p in range(per)], axis=1
            )
            next_ref[:, at] = jnp.concatenate(
                [own[i * per + p].astype(next_ref.dtype) for p in range(per)], axis=1
            )
            pre = dot(w_ref[...], agg, ((1,), (0,))) + dot(b_ref[...], x_ref[:, at], ((1,), (0,)))
            fixed_ref[:, at] = jnp.maximum(pre, 0.0).astype(fixed_ref.dtype)
            adj = adj_ref[:, at]
            masked = jnp.where(z_ref[:, at] > 0, adj, jnp.zeros_like(adj))
            wg_ref[...] += dot(masked, agg, ((1,), (1,)))
            return c

        lax.fori_loop(0, nodes // LANES, chunk, 0)


def reduce_kernel(
    n, rows, scale, wg_in, ig_in, wg_out, ig_out, part, slots, total, done, s1, r1, s2, r2
):
    me = lax.axis_index("dom")
    height, width = wg_in.shape
    pieces = part.shape[0] // rows
    barrier = pltpu.get_barrier_semaphore()

    def other(j):
        return lax.rem(me + j, n)

    def greet(j, c):
        pl.semaphore_signal(barrier, inc=1, device_id=(other(j),), device_id_type=MESH)
        return c

    lax.fori_loop(1, n, greet, 0)
    part[...] = jnp.zeros_like(part)
    part[0:height, 0:width] = wg_in[...]
    part[height : 2 * height, 0 : ig_in.shape[1]] = ig_in[...]
    pl.semaphore_wait(barrier, n - 1)

    def first(p):
        return pltpu.make_async_remote_copy(
            src_ref=part.at[pl.ds(pl.multiple_of(p * rows, rows), rows)],
            dst_ref=slots.at[me],
            send_sem=s1.at[p],
            recv_sem=r1.at[me],
            device_id=(p,),
            device_id_type=MESH,
        )

    def arrived(d):
        return pltpu.make_async_remote_copy(
            src_ref=slots.at[d],
            dst_ref=slots.at[d],
            send_sem=s1.at[0],
            recv_sem=r1.at[d],
            device_id=(d,),
            device_id_type=MESH,
        )

    def second(d):
        at = pl.ds(pl.multiple_of(me * rows, rows), rows)
        return pltpu.make_async_remote_copy(
            src_ref=total,
            dst_ref=done.at[at],
            send_sem=s2.at[d],
            recv_sem=r2.at[me],
            device_id=(d,),
            device_id_type=MESH,
        )

    def second_in(p):
        at = pl.ds(pl.multiple_of(p * rows, rows), rows)
        return pltpu.make_async_remote_copy(
            src_ref=total,
            dst_ref=done.at[at],
            send_sem=s2.at[0],
            recv_sem=r2.at[p],
            device_id=(p,),
            device_id_type=MESH,
        )

    def each(count, action):
        def body(i, c):
            @pl.when(i != me)
            def _():
                action(i)

            return c

        lax.fori_loop(0, count, body, 0)

    each(pieces, lambda p: first(p).start())

    @pl.when(me < pieces)
    def _():
        own = pl.ds(pl.multiple_of(me * rows, rows), rows)
        slots[me] = part[own]
        each(n, lambda d: arrived(d).wait_recv())
        total[...] = jnp.zeros_like(total)

        def add(d, c):
            total[...] += slots[d]
            return c

        lax.fori_loop(0, n, add, 0)
        each(n, lambda d: second(d).start())
        done[own] = total[...]

    each(pieces, lambda p: second_in(p).wait_recv())
    wg_out[...] = done[0:height, 0:width] * scale
    ig_out[...] = done[height : 2 * height, 0 : ig_in.shape[1]] * scale
    each(pieces, lambda p: first(p).wait_send())

    @pl.when(me < pieces)
    def _():
        each(n, lambda d: second(d).wait_send())


def whole(array_shape):
    return pl.BlockSpec(
        array_shape, lambda i, *_: (0,) * len(array_shape), pipeline_mode=pl.Buffered(1)
    )


def per_device(
    n, z_state, inputs, adjoint, cotangent, mix_weight, input_weight, tile_values, tile_src,
    tile_dst, send_list,
):
    channels, nodes = z_state.shape
    features = inputs.shape[0]
    stored, tile, _ = tile_values.shape
    local_tiles = nodes // tile
    _, peers, cap = send_list.shape
    slots = peers * cap
    reach = peers // 2
    offsets = [r + 1 for r in range(reach)] + [-(r + 1) for r in range(reach)]
    src, dst, send = tile_src[0], tile_dst[0], send_list.reshape(-1)
    f32, bf16 = jnp.float32, jnp.bfloat16
    sds = jax.ShapeDtypeStruct
    a_spec = pl.BlockSpec((BLOCK, tile, tile), lambda i, *_: (i, 0, 0))
    piece = (channels, tile)
    wide = whole((channels, nodes))

    zout, leave, local, ig = pl.pallas_call(
        backward_kernel,
        name="backward",
        out_shape=(
            sds((slots,) + piece, bf16),
            sds((slots,) + piece, bf16),
            sds((local_tiles,) + piece, f32),
            sds((channels, features), f32),
        ),
        grid_spec=pltpu.PrefetchScalarGridSpec(
            num_scalar_prefetch=3,
            grid=(stored // BLOCK,),
            in_specs=[wide, wide, whole((features, nodes)), whole(mix_weight.shape), a_spec],
            out_specs=[
                whole((slots,) + piece),
                whole((slots,) + piece),
                whole((local_tiles,) + piece),
                whole((channels, features)),
            ],
            scratch_shapes=[
                pltpu.VMEM((channels, nodes), bf16),
                pltpu.VMEM((local_tiles + slots,) + piece, f32),
            ],
        ),
    )(src, dst, send, z_state, adjoint, inputs, mix_weight, tile_values)

    any_spec = pl.BlockSpec(memory_space=pl.ANY)
    zin, ret = pl.pallas_call(
        functools.partial(exchange_kernel, n, offsets),
        name="exchange",
        out_shape=(sds((slots,) + piece, bf16), sds((slots,) + piece, bf16)),
        in_specs=[any_spec] * 2,
        out_specs=(any_spec, any_spec),
        scratch_shapes=[
            pltpu.SemaphoreType.DMA((2, peers)),
            pltpu.SemaphoreType.DMA((2, peers)),
        ],
        compiler_params=pltpu.CompilerParams(collective_id=0, has_side_effects=True),
    )(zout, leave)

    fixed_next, adjoint_next, wg = pl.pallas_call(
        forward_kernel,
        name="forward",
        out_shape=(
            sds((channels, nodes), bf16),
            sds((channels, nodes), bf16),
            sds((channels, channels), f32),
        ),
        grid_spec=pltpu.PrefetchScalarGridSpec(
            num_scalar_prefetch=3,
            grid=(stored // BLOCK,),
            in_specs=[
                wide,
                wide,
                wide,
                whole((features, nodes)),
                whole(mix_weight.shape),
                whole(input_weight.shape),
                whole((slots,) + piece),
                whole((slots,) + piece),
                whole((local_tiles,) + piece),
                a_spec,
            ],
            out_specs=[wide, wide, whole((channels, channels))],
            scratch_shapes=[
                pltpu.VMEM((local_tiles + slots,) + piece, bf16),
                pltpu.VMEM((local_tiles,) + piece, f32),
                pltpu.VMEM((local_tiles,) + piece, f32),
            ],
        ),
    )(
        src, dst, send, z_state, adjoint, cotangent, inputs, mix_weight, input_weight, zin, ret,
        local, tile_values,
    )

    width = max(channels, features)
    units = -(-2 * channels // 8)
    rows = 8 * -(-units // n)
    pieces = -(-2 * channels // rows)
    vmem = pl.BlockSpec(memory_space=pltpu.VMEM)
    scale = 1.0 / math.sqrt(nodes * n)
    weight_grad, input_grad = pl.pallas_call(
        functools.partial(reduce_kernel, n, rows, scale),
        name="reduce",
        out_shape=(sds((channels, channels), f32), sds((channels, features), f32)),
        in_specs=[vmem] * 2,
        out_specs=(vmem, vmem),
        scratch_shapes=[
            pltpu.VMEM((pieces * rows, width), f32),
            pltpu.VMEM((n, rows, width), f32),
            pltpu.VMEM((rows, width), f32),
            pltpu.VMEM((pieces * rows, width), f32),
            pltpu.SemaphoreType.DMA((pieces,)),
            pltpu.SemaphoreType.DMA((n,)),
            pltpu.SemaphoreType.DMA((n,)),
            pltpu.SemaphoreType.DMA((pieces,)),
        ],
        compiler_params=pltpu.CompilerParams(collective_id=1, has_side_effects=True),
    )(wg, ig)
    return fixed_next, adjoint_next, weight_grad, input_grad


def solution(mesh):
    return jax.shard_map(
        functools.partial(per_device, mesh.shape["dom"]),
        mesh=mesh,
        in_specs=(
            P(None, "dom"),
            P(None, "dom"),
            P(None, "dom"),
            P(None, "dom"),
            P(),
            P(),
            P("dom", None, None),
            P("dom", None),
            P("dom", None),
            P("dom", None, None),
        ),
        out_specs=(P(None, "dom"), P(None, "dom"), P(), P()),
        check_vma=False,
    )
```

time: 489 us -> 162 us (0.33)
  the two profiles are of different devices: /device:TPU:2 before, /device:TPU:4 now
where the time goes in v1:
time: 162 us; the launch traced here: 159 us
  Pallas kernels  154 us (95%)
  local copies, waits for them, and re-layouts  4.2 us (3%)
    pallas_call x1, Pallas kernels, per_device(): pl.pallas_call(functools.partial(exchange_kernel, n, offsets), name='exch...  86.9 us
    pallas_call x1, Pallas kernels, per_device(): pl.pallas_call(backward_kernel, name='backward', out_shape=(sds((slots,)...  25.5 us
    pallas_call x1, Pallas kernels, per_device(): pl.pallas_call(forward_kernel, name='forward', out_shape=(sds((channels,...  23.9 us
    pallas_call x1, Pallas kernels, per_device(): pl.pallas_call(functools.partial(reduce_kernel, n, rows, scale), name='re...  18.1 us

profile of v1, /device:TPU:4, one launch (start us, length us, event | category | flops | bytes accessed | tf_op | source)
XLA Modules:
  0.0 159.3 jit_solution(2679929565741361499)
XLA Ops:
  0.6 1.4 reshape.11.send
  2.0 25.5 %backward.1 = (bf16[128,96,128]{2,1,0:T(8,128)(2,1)}, bf16[128,96,128]{2,1,0:T(8,128)(2,1)}, f32[64,96,128]{2,1,0:T(8,128)}, f32[96,128]{1,0:T(8,128)}) custom-call(s32[256]{0:T(256)} %bitcast.2, s32[256]{0:T(256)} %bitcast.4, s32[128]{0:T(128)} %reshape.11.send, bf16[96,8192]{1,0:T(8,128)(2,1)} %z_ref.3, bf16[96,8192]{1,0:T(8,128)(2,1)} %adj_ref.3, ...), custom_call_target="tpu_custom_call" | custom-call | tf_op jit(solution)/shard_map/backward/pallas_call | solution.py:288
  27.5 86.9 %exchange.1 = (bf16[128,96,128]{2,1,0:T(8,128)(2,1)}, bf16[128,96,128]{2,1,0:T(8,128)(2,1)}) custom-call(bf16[128,96,128]{2,1,0:T(8,128)(2,1)} %get-tuple-element.15.zout, bf16[128,96,128]{2,1,0:T(8,128)(2,1)} %get-tuple-element.16.leave), custom_call_target="tpu_custom_call" | custom-call | tf_op jit(solution)/shard_map/exchange/pallas_call | solution.py:315
  114.4 23.9 %forward.1 = (bf16[96,8192]{1,0:T(8,128)(2,1)}, bf16[96,8192]{1,0:T(8,128)(2,1)}, f32[96,96]{1,0:T(8,128)}) custom-call(s32[256]{0:T(256)} %bitcast.3, s32[256]{0:T(256)} %bitcast.5, s32[128]{0:T(128)} %reshape.11.send, bf16[96,8192]{1,0:T(8,128)(2,1)} %z_ref.3, bf16[96,8192]{1,0:T(8,128)(2,1)} %adj_ref.3, bf16[96,8192]{1,0:T(8,128)(2,1)} %cot_ref.1, ...), custom_call_target="tpu_custom_call" | custom-call | tf_op jit(solution)/shard_map/forward/pallas_call | solution.py:328
  138.3 18.1 %reduce.1 = (f32[96,96]{1,0:T(8,128)}, f32[96,128]{1,0:T(8,128)}) custom-call(f32[96,96]{1,0:T(8,128)} %get-tuple-element.22.wg_in, f32[96,128]{1,0:T(8,128)} %get-tuple-element.23.ig_in), custom_call_target="tpu_custom_call" | custom-call | tf_op jit(solution)/shard_map/reduce/pallas_call | solution.py:369
  156.5 1.4 copy.16
  157.9 1.4 copy.17
